TPU v7x, 1024 devices: a whole 4x8x16 slice. The times are simulated.
1024 devices in a mesh: board: 256 (over y, z, core), seq: 4 (over x).
Axes of the slice: x: 4, y: 8, z: 16, core: 2. Of those that a mesh axis runs over, the one named last changes fastest.
Arguments:
- board_cards: int32 [256, 6, 5], P('board'), may hold values from 0 to 51, as said below
- hand_ranks: int32 [256, 6, 1326], P('board'), may hold values from 0 to 7461
- river_count: int32 [256], P('board'), may hold values from 1 to 6, as said below
- reach_in: bfloat16 [256, 24, 1326], P('board', 'seq'), may hold values from 0 to 1
- strategy: bfloat16 [256, 6, 192, 1326], P('board', None, 'seq'), may hold values from 0.049804688 to 1
- parent_node: int32 [192], P('seq'), may hold values from 0 to 23, as said below
- pot_size: float32 [192], P('seq'), may hold values from 0.5 to 4
- flop_weight: float32 [256], P('board'), may hold values from 0.1 to 10
Outputs:
- turn_value: float32 [256, 24, 1326], P('board', 'seq')
- root_value: float32 [24, 1326], P('seq')
Inputs may be any that keep to these rules, and one draw needn't show every extreme that they name: `board_cards`: the five cards of a river board are distinct; the first three are the flop group's and the same on all of its river boards. `river_count`: some flop group has 6 live river boards; slots at or past the count hold unused data. `parent_node`: each river root is the parent of exactly 8 leaves.
All inputs are finite; a program needn't handle non-finite values.
Results may differ from a plain program's by a relative error of at most 0.0003.
Values may be sent and summed in bfloat16 or wider, within the bound.
A program may use at most 32 MiB of HBM per device.

v0:
```python
import jax
import jax.numpy as jnp
import numpy as np
from jax import lax
from jax.sharding import PartitionSpec as P

DECK = 52
HANDS = 1326
NODES = 24


lowest = -1000000000.0


def hand_tables():
    card_low, card_high = np.triu_indices(DECK, 1)
    return (jnp.asarray(card_low, jnp.int32), jnp.asarray(card_high, jnp.int32))


def unblocked_mask(board_row, card_low, card_high):
    card_hit = (card_low[:, None] == board_row[None, :]) | (
        card_high[:, None] == board_row[None, :]
    )
    return jnp.where(jnp.any(card_hit, axis=1), 0.0, 1.0).astype(jnp.float32)


def river_nodes(board_row, ranking, strat_rows, reach_rows, member, pot_size, card_low, card_high):
    hand_live = unblocked_mask(board_row, card_low, card_high)
    lookup = jnp.dot(member.astype(jnp.bfloat16), reach_rows, preferred_element_type=jnp.float32)
    leaf_reach = (lookup * strat_rows * hand_live[None, :]).astype(jnp.bfloat16)
    block_width = HANDS // 3

    def add_block(block_index, showdown):
        block_start = block_index * block_width
        rank_block = lax.dynamic_slice_in_dim(ranking, block_start, block_width)
        low_block = lax.dynamic_slice_in_dim(card_low, block_start, block_width)
        high_block = lax.dynamic_slice_in_dim(card_high, block_start, block_width)
        shared_card = (
            (low_block[:, None] == card_low[None, :])
            | (low_block[:, None] == card_high[None, :])
            | (high_block[:, None] == card_low[None, :])
            | (high_block[:, None] == card_high[None, :])
        )
        payoff_rows = jnp.where(
            shared_card, 0, jnp.sign(ranking[None, :] - rank_block[:, None])
        ).astype(jnp.bfloat16)
        reach_block = lax.dynamic_slice_in_dim(leaf_reach, block_start, block_width, 1)
        return showdown + jnp.dot(reach_block, payoff_rows, preferred_element_type=jnp.float32)

    showdown = lax.fori_loop(0, 3, add_block, jnp.zeros((strat_rows.shape[0], HANDS), jnp.float32))
    leaf_value = pot_size[:, None] * showdown * hand_live[None, :] / HANDS

    def one_node(column):
        return jnp.max(jnp.where(column[:, None], leaf_value, lowest), axis=0)

    return lax.map(one_node, member.T)


def fill_values(
    board_rows,
    rank_rows,
    strat_all,
    reach_all,
    member,
    pot_size,
    card_low,
    card_high,
    slot_of,
    item_start,
    item_stop,
):
    rivers = rank_rows.shape[0] // reach_all.shape[0]
    initial = jnp.full((rivers, NODES, HANDS), lowest, jnp.float32)

    def fill_slot(item_index, buffer):
        slot_index = slot_of(item_index)
        values = river_nodes(
            lax.dynamic_index_in_dim(board_rows, slot_index, 0, keepdims=False),
            lax.dynamic_index_in_dim(rank_rows, slot_index, 0, keepdims=False),
            lax.dynamic_index_in_dim(strat_all, slot_index, 0, keepdims=False),
            lax.dynamic_index_in_dim(reach_all, slot_index // rivers, 0, keepdims=False),
            member,
            pot_size,
            card_low,
            card_high,
        )
        return lax.dynamic_update_slice(buffer, values[None], (item_index - item_start, 0, 0))

    return lax.fori_loop(item_start, item_stop, fill_slot, initial)


def node_part(buffer):
    seq_count = lax.axis_size("seq")
    part_width = NODES // seq_count
    merged = lax.pmax(buffer, "seq")
    return lax.dynamic_slice_in_dim(merged, lax.axis_index("seq") * part_width, part_width, 1)


def body(
    board_cards, hand_ranks, river_count, reach_in, strategy, parent_node, pot_size, flop_weight
):
    card_low, card_high = hand_tables()
    member = parent_node[:, None] == jnp.arange(NODES, dtype=jnp.int32)[None, :]
    reach_all = lax.all_gather(reach_in, "seq", axis=1, tiled=True)
    rivers = hand_ranks.shape[1]
    live_count = river_count[0]
    buffer = fill_values(
        board_cards[0],
        hand_ranks[0],
        strategy[0],
        reach_all,
        member,
        pot_size,
        card_low,
        card_high,
        lambda item_index: item_index,
        0,
        live_count,
    )
    node_values = node_part(buffer)
    river_live = jnp.arange(rivers, dtype=jnp.int32) < live_count
    summed = jnp.sum(jnp.where(river_live[:, None, None], node_values, 0.0), axis=0)
    turn_share = summed / live_count.astype(jnp.float32)
    root_total = lax.psum(flop_weight[0] * turn_share / lax.axis_size("board"), "board")
    return (turn_share[None], root_total)


def solution(mesh):
    return jax.shard_map(
        body,
        mesh=mesh,
        in_specs=(
            P("board", None, None),
            P("board", None, None),
            P("board"),
            P("board", "seq", None),
            P("board", None, "seq", None),
            P("seq"),
            P("seq"),
            P("board"),
        ),
        out_specs=(P("board", "seq", None), P("seq", None)),
        check_vma=False,
    )
```

profile of v0, /device:TPU:1, one launch (start us, length us, event | category | flops | bytes accessed | tf_op | source)
XLA Modules:
  0.0 1179.8 jit_solution(12004692338365521473)
XLA Ops:
  7.3 0.8 copy.21
  8.0 0.8 copy.16
  8.8 10.3 all_gather.3
  19.1 0.8 copy.17
  20.0 16.3 %while.45 = (s32[]{:T(128)}, f32[6,24,1326]{2,1,0:T(8,128)S(1)}, s32[]{:T(128)}, f32[48]{0:T(128)S(1)}, s32[6,1326]{1,0:T(8,128)S(1)}, /*index=5*/bf16[1,24,1326...) while((s32[]{:T(128)}, f32[6,24,1326]{2,1,0:T(8,128)S(1)}, ...), condition=%wide.region_7.8_spmd.clone.clone, body=%wide.region_0.7_spmd.sunk.clone.clone.sunk | while | flops 66494584 | bytes 2036673 | solution.py:89
  20.8 1.2 fusion.24
  22.0 6.0 while.46
  22.2 1.7 convolution_add_fusion.2
  24.2 1.7 convolution_add_fusion.2
  26.2 1.7 convolution_add_fusion.2
  28.1 7.5 while.47
  28.1 0.1 select_reduce_fusion.3
  28.2 0.1 dynamic_update_slice.14
  28.4 0.1 select_reduce_fusion.3
  28.5 0.1 dynamic_update_slice.14
  28.7 0.1 select_reduce_fusion.3
  28.9 0.1 dynamic_update_slice.14
  29.0 0.1 select_reduce_fusion.3
  29.2 0.1 dynamic_update_slice.14
  29.4 0.1 select_reduce_fusion.3
  29.5 0.1 dynamic_update_slice.14
  29.7 0.1 select_reduce_fusion.3
  29.8 0.1 dynamic_update_slice.14
  30.0 0.1 select_reduce_fusion.3
  30.1 0.1 dynamic_update_slice.14
  30.3 0.1 select_reduce_fusion.3
  30.4 0.1 dynamic_update_slice.14
  30.6 0.1 select_reduce_fusion.3
  30.7 0.1 dynamic_update_slice.14
  30.9 0.1 select_reduce_fusion.3
  31.0 0.1 dynamic_update_slice.14
  31.2 0.1 select_reduce_fusion.3
  31.3 0.1 dynamic_update_slice.14
  31.5 0.1 select_reduce_fusion.3
  31.7 0.1 dynamic_update_slice.14
  31.8 0.1 select_reduce_fusion.3
  32.0 0.1 dynamic_update_slice.14
  32.2 0.1 select_reduce_fusion.3
  32.3 0.1 dynamic_update_slice.14
  32.5 0.1 select_reduce_fusion.3
  32.6 0.1 dynamic_update_slice.14
  32.8 0.1 select_reduce_fusion.3
  32.9 0.1 dynamic_update_slice.14
  33.1 0.1 select_reduce_fusion.3
  33.2 0.1 dynamic_update_slice.14
  33.4 0.1 select_reduce_fusion.3
  33.5 0.1 dynamic_update_slice.14
  33.7 0.1 select_reduce_fusion.3
  33.8 0.1 dynamic_update_slice.14
  34.0 0.1 select_reduce_fusion.3
  34.2 0.1 dynamic_update_slice.14
  34.3 0.1 select_reduce_fusion.3
  34.5 0.1 dynamic_update_slice.14
  34.7 0.1 select_reduce_fusion.3
  34.8 0.1 dynamic_update_slice.14
  35.0 0.1 select_reduce_fusion.3
  35.1 0.1 dynamic_update_slice.14
  35.3 0.1 select_reduce_fusion.3
  35.4 0.1 dynamic_update_slice.14
  36.2 0.9 copy-done
  38.5 150.6 %all-reduce.2.cloned.1.call-done = f32[6,24,1326]{2,1,0:T(8,128)} async-done(((f32[6,24,1326]{2,1,0:T(8,128)}), f32[6,24,1326]{2,1,0:T(8,128)}) %all-reduce.2.cloned.1.call-update) | async-done | bytes 763792 | tf_op jit(solution)/shard_map/pmax | solution.py:95
  189.1 1.2 select_reduce_fusion.1
  190.3 0.6 div.29
  190.9 982.0 %psum.7 = f32[6,1326]{1,0:T(8,128)} all-reduce(f32[6,1326]{1,0:T(8,128)S(1)} %get-tuple-element.341), channel_id=1, replica_groups=mesh['board'=256,'seq'=4] {'board'}, use_global_device_ids=true, to_apply=%region_10.11 | all-reduce | flops 7956 | bytes 63648 | tf_op jit(solution)/shard_map/psum | solution.py:124
  (81 shorter events, 1.6 us)
Async XLA Ops:
  7.2 12.8 %copy-start.1 = (s32[1326]{0:T(1024)S(1)}, s32[1326]{0:T(1024)}, u32[]{:S(2)}) copy-start(s32[1326]{0:T(1024)} %constant.100.clone..sunk.3) | copy-start | bytes 15916
  7.2 12.8 %copy-start.2 = (s32[1326]{0:T(1024)S(1)}, s32[1326]{0:T(1024)}, u32[]{:S(2)}) copy-start(s32[1326]{0:T(1024)} %constant.99.clone..sunk.3) | copy-start | bytes 15916
  7.2 12.8 %copy-start.4 = (f32[48]{0:T(128)S(1)}, f32[48]{0:T(128)}, u32[]{:S(2)}) copy-start(f32[48]{0:T(128)} %param.22) | copy-start | bytes 580
  7.2 12.8 %copy-start.3 = (s32[48]{0:T(128)S(1)}, s32[48]{0:T(128)}, u32[]{:S(2)}) copy-start(s32[48]{0:T(128)} %param.21) | copy-start | bytes 580
  7.2 181.9 %all-reduce.2.cloned.1.call-start = ((), (), s32[]{:S(2)}) async-start(), calls=%async_computation | async-start | bytes 1622016 | tf_op jit(solution)/shard_map/pmax | solution.py:95
  36.2 0.9 copy-start
Sparse Core Ops, SparseCore 0:
  37.3 151.7 all-reduce.1
where the time goes:
time: 1180 us
  blocking collectives  992 us (84%)
  waiting for transfers between devices  151 us (13%)
  between operations  15.4 us (1%)
    psum x1, blocking collectives, body(): lax.psum(flop_weight[0] * turn_share / lax.axis_size('board'), 'board')  982 us
    pmax x1, waiting for transfers between devices, node_part(): merged = lax.pmax(buffer, 'seq')  151 us
  transfers between devices with their start and end apart: 1, of which 1 were waited for; matrix products, arithmetic and copies ran while one was open for 0% of the time, Pallas kernels for 0%

commit v1 on v0

v1 whole, which is shorter than its diff:
```python
import jax
import jax.numpy as jnp
import numpy as np
from jax import lax
from jax.experimental import pallas as pl
from jax.experimental.pallas import tpu as pltpu
from jax.sharding import PartitionSpec as P

HANDS, NODES, RIVERS, LEAF = 1326, 24, 6, 48
NX, NY, NZ, NC = 4, 8, 16, 2
GROUP = NY * NC
SLOTS = 8 * NODES
PART = NODES // NX
TILES = -(-HANDS // 128)
lowest = -1000000000.0
MESH = pl.DeviceIdType.MESH
VM = pl.BlockSpec(memory_space=pltpu.VMEM)
SM = pl.BlockSpec(memory_space=pltpu.SMEM)
f32, bf16 = jnp.float32, jnp.bfloat16


def seq_peer(d):
    return (lax.axis_index("board"), lax.rem(lax.axis_index("seq") + d, NX))


def place():
    board = lax.axis_index("board")
    core = lax.rem(board, NC)
    z = lax.rem(board // NC, NZ)
    return board // (NC * NZ), z, core


def group_peer(d):
    y, z, core = place()
    g = lax.rem(y * NC + core + d, GROUP)
    return ((g // NC * NZ + z) * NC + lax.rem(g, NC), lax.axis_index("seq"))


def line_peer(d):
    y, z, core = place()
    return ((y * NZ + lax.rem(z + d, NZ)) * NC + core, lax.axis_index("seq"))


def meet(peers):
    barrier = pltpu.get_barrier_semaphore()
    for peer in peers:
        pl.semaphore_signal(barrier, inc=1, device_id=peer, device_id_type=MESH)
    pl.semaphore_wait(barrier, len(peers))


def send(src, dst, send_sem, recv_sem, peer):
    copy = pltpu.make_async_remote_copy(
        src_ref=src, dst_ref=dst, send_sem=send_sem, recv_sem=recv_sem, device_id=peer, device_id_type=MESH
    )
    copy.start()
    return copy


def gather_kernel(reach_ref, out_ref, got_ref, send_sem, recv_sem):
    meet([seq_peer(d) for d in range(1, NX)])
    x = lax.axis_index("seq")
    copies = [
        send(reach_ref.at[0], got_ref.at[x], send_sem.at[d], recv_sem.at[d], seq_peer(d)) for d in range(1, NX)
    ]
    got_ref[x] = reach_ref[0]
    for copy in copies:
        copy.wait()
    for x in range(NX):
        out_ref[PART * x : PART * (x + 1), :] = got_ref[x].astype(f32)


def gather(reach):
    return pl.pallas_call(
        gather_kernel,
        name="gather_reach",
        out_shape=jax.ShapeDtypeStruct((NODES, HANDS), f32),
        in_specs=[VM],
        out_specs=VM,
        scratch_shapes=[
            pltpu.VMEM((NX, PART, HANDS), bf16),
            pltpu.SemaphoreType.DMA((NX,)),
            pltpu.SemaphoreType.DMA((NX,)),
        ],
        compiler_params=pltpu.CompilerParams(collective_id=0, has_side_effects=True),
    )(reach)


def compute_kernel(
    cards_ref,
    ranks_ref,
    count_ref,
    reach_ref,
    strat_ref,
    parow_ref,
    pacol_ref,
    pot_ref,
    tab_ref,
    out_ref,
    m_ref,
    row_ref,
    col_ref,
    oh_ref,
    potb_ref,
    biasb_ref,
    scale_ref,
):
    low = tab_ref[0:1, :]
    high = tab_ref[1:2, :]
    card = lax.broadcasted_iota(jnp.int32, (64, HANDS), 0)
    onehot = jnp.where((card == low) | (card == high), 1.0, 0.0).astype(bf16)
    for j in range(0, HANDS, 256):
        w = min(256, HANDS - j)
        shared = lax.dot_general(
            onehot, onehot[:, j : j + w], (((0,), (0,)), ((), ())), preferred_element_type=f32
        )
        m_ref[:, j : j + w] = (1.0 - jnp.minimum(shared, 1.0)).astype(bf16)
    ranks = ranks_ref[...]
    top = ranks // 128
    row_ref[0, 0:RIVERS, :] = (top * 128).astype(f32)
    row_ref[1, 0:RIVERS, :] = (ranks - top * 128).astype(f32)
    col_ref[0] = row_ref[0].T
    col_ref[1] = row_ref[1].T
    cards = cards_ref[...]
    hit = jnp.zeros((RIVERS, HANDS), jnp.bool_)
    for i in range(5):
        hit = hit | (low == cards[:, i : i + 1]) | (high == cards[:, i : i + 1])
    dead = lax.broadcasted_iota(jnp.int32, (RIVERS, HANDS), 0) >= count_ref[0]
    share = 1.0 / (HANDS * jnp.full((RIVERS, HANDS), count_ref[0], jnp.int32).astype(f32))
    scale_ref[0:RIVERS, :] = jnp.where(hit, 0.0, 1.0)
    scale_ref[8 : 8 + RIVERS, :] = jnp.where(hit | dead, 0.0, share)
    prow = parow_ref[...]
    pcol = pacol_ref[...]
    si = lax.broadcasted_iota(jnp.int32, (LEAF, LEAF), 0)
    sj = lax.broadcasted_iota(jnp.int32, (LEAF, LEAF), 1)
    before = jnp.sum(jnp.where((prow == pcol) & (si < sj), 1.0, 0.0), axis=0, keepdims=True).astype(jnp.int32)
    oh = lax.broadcasted_iota(jnp.int32, (SLOTS, LEAF), 0) == before * NODES + prow
    oh_ref[...] = jnp.where(oh, 1.0, 0.0).astype(bf16)
    pot = jnp.sum(jnp.where(oh, pot_ref[...], 0.0), axis=1, keepdims=True)
    used = jnp.sum(jnp.where(oh, 1.0, 0.0), axis=1, keepdims=True)
    potb_ref[...] = jnp.broadcast_to(pot, (SLOTS, 128))
    biasb_ref[...] = jnp.broadcast_to(jnp.where(used > 0.5, 0.0, lowest), (SLOTS, 128))

    reach = reach_ref[...]
    pot2 = jnp.concatenate([potb_ref[...]] * 2, axis=1)
    bias2 = jnp.concatenate([biasb_ref[...]] * 2, axis=1)
    for r in range(RIVERS):
        leaf = jnp.dot(oh_ref[...], strat_ref[r], preferred_element_type=f32).reshape(8, NODES, HANDS)
        leaf = (leaf * (reach * scale_ref[r : r + 1, :])[None]).reshape(SLOTS, HANDS).astype(bf16)
        hc = jnp.broadcast_to(col_ref[0, :HANDS, r : r + 1], (HANDS, 256)).astype(bf16)
        lc = jnp.broadcast_to(col_ref[1, :HANDS, r : r + 1], (HANDS, 256)).astype(bf16)
        for j in range(0, HANDS, 256):
            w = min(256, HANDS - j)
            hr = row_ref[0, r : r + 1, j : j + w].astype(bf16)
            lr = row_ref[1, r : r + 1, j : j + w].astype(bf16)
            gap = (hr - hc[:, :w]) + (lr - lc[:, :w])
            m = m_ref[:, j : j + w]
            payoff = jnp.maximum(jnp.minimum(gap, m), -m)
            val = jnp.dot(leaf, payoff, preferred_element_type=f32)
            val = (val * pot2[:, :w] + bias2[:, :w]).reshape(8, NODES, w)
            best = jnp.max(val, axis=0) * scale_ref[8 + r : 9 + r, j : j + w]
            for x in range(NX):
                out_ref[x, r, :, j : j + w] = best[PART * x : PART * (x + 1)]


def compute(cards, ranks, count, reach, strat, parent, pot):
    tab = jnp.asarray(np.stack(np.triu_indices(52, 1)), jnp.int32)
    return pl.pallas_call(
        compute_kernel,
        name="river_maxima",
        out_shape=jax.ShapeDtypeStruct((NX, RIVERS, PART, HANDS), f32),
        in_specs=[VM, VM, SM, VM, VM, VM, VM, VM, VM],
        out_specs=VM,
        scratch_shapes=[
            pltpu.VMEM((HANDS, HANDS), bf16),
            pltpu.VMEM((2, 8, HANDS), f32),
            pltpu.VMEM((2, HANDS, 8), f32),
            pltpu.VMEM((SLOTS, LEAF), bf16),
            pltpu.VMEM((SLOTS, 128), f32),
            pltpu.VMEM((SLOTS, 128), f32),
            pltpu.VMEM((16, HANDS), f32),
        ],
        compiler_params=pltpu.CompilerParams(vmem_limit_bytes=48 << 20),
    )(cards, ranks, count, reach, strat, parent[None, :], parent[:, None], pot[None, :], tab)


def reduce_kernel(
    part_ref, weight_ref, turn_ref, root_ref, got_ref, mine_ref, in1_ref, sum1_ref, in2_ref, sum2_ref, in3_ref,
    sx, rx, s1, r1, s2, r2, s3, r3,
):
    meet(
        [seq_peer(d) for d in range(1, NX)]
        + [group_peer(d) for d in range(1, GROUP)]
        + [line_peer(d) for d in range(1, NZ)]
    )
    x = lax.axis_index("seq")
    y, z, core = place()
    g = y * NC + core
    copies = [
        send(part_ref.at[lax.rem(x + d, NX)], got_ref.at[d], sx.at[d], rx.at[d], seq_peer(d)) for d in range(1, NX)
    ]
    mine_ref[...] = jnp.zeros_like(mine_ref)
    for copy in copies:
        copy.wait()
    best = jnp.maximum(jnp.maximum(part_ref[x], got_ref[1]), jnp.maximum(got_ref[2], got_ref[3])) if NX == 4 else jnp.maximum(part_ref[x], got_ref[1])
    turn = jnp.sum(best, axis=0)
    turn_ref[...] = turn
    turn = turn * (weight_ref[0] / (NY * NZ * NC))
    for j in range(TILES):
        w = min(128, HANDS - 128 * j)
        mine_ref[j, 0:PART, 0:w] = turn[:, 128 * j : 128 * j + w]
    copies = [
        send(mine_ref.at[lax.rem(g + d, GROUP)], in1_ref.at[d], s1.at[d], r1.at[d], group_peer(d))
        for d in range(1, GROUP)
    ]
    total = mine_ref[g]
    for d in range(1, GROUP):
        copies[d - 1].wait_recv()
        total = total + in1_ref[d]
    sum1_ref[...] = total
    for copy in copies:
        copy.wait_send()
    copies = [send(sum1_ref, in2_ref.at[z], s2.at[d], r2.at[d], line_peer(d)) for d in range(1, NZ)]
    in2_ref[z] = total
    for copy in copies:
        copy.wait()
    sum2_ref[...] = jnp.sum(in2_ref[...], axis=0)
    copies = [send(sum2_ref, in3_ref.at[g], s3.at[d], r3.at[d], group_peer(d)) for d in range(1, GROUP)]
    in3_ref[g] = sum2_ref[...]
    for copy in copies:
        copy.wait()
    for j in range(TILES):
        w = min(128, HANDS - 128 * j)
        root_ref[:, 128 * j : 128 * j + w] = in3_ref[j, 0:PART, 0:w]


def reduce(part, weight):
    tile = (8, 128)
    sems = [pltpu.SemaphoreType.DMA((n,)) for n in (NX, NX, GROUP, GROUP, NZ, NZ, GROUP, GROUP)]
    return pl.pallas_call(
        reduce_kernel,
        name="exchange_reduce",
        out_shape=(jax.ShapeDtypeStruct((PART, HANDS), f32), jax.ShapeDtypeStruct((PART, HANDS), f32)),
        in_specs=[VM, SM],
        out_specs=(VM, VM),
        scratch_shapes=[
            pltpu.VMEM((NX, RIVERS, PART, HANDS), f32),
            pltpu.VMEM((GROUP,) + tile, f32),
            pltpu.VMEM((GROUP,) + tile, f32),
            pltpu.VMEM(tile, f32),
            pltpu.VMEM((NZ,) + tile, f32),
            pltpu.VMEM(tile, f32),
            pltpu.VMEM((GROUP,) + tile, f32),
        ]
        + sems,
        compiler_params=pltpu.CompilerParams(collective_id=1, has_side_effects=True),
    )(part, weight)


def body(
    board_cards, hand_ranks, river_count, reach_in, strategy, parent_node, pot_size, flop_weight
):
    reach = gather(reach_in)
    part = compute(board_cards[0], hand_ranks[0], river_count, reach, strategy[0], parent_node, pot_size)
    turn, root = reduce(part, flop_weight)
    return (turn[None], root)


def solution(mesh):
    return jax.shard_map(
        body,
        mesh=mesh,
        in_specs=(
            P("board", None, None),
            P("board", None, None),
            P("board"),
            P("board", "seq", None),
            P("board", None, "seq", None),
            P("seq"),
            P("seq"),
            P("board"),
        ),
        out_specs=(P("board", "seq", None), P("seq", None)),
        check_vma=False,
    )
```

time: 1180 us -> 86.9 us (0.07)
  blocking collectives: 992 us -> 0 us
  waiting for transfers between devices: 151 us -> 0 us
  Pallas kernels: 0 us -> 74.1 us
  between operations: 15.4 us -> 1.98 us
    psum x1 -> x0, blocking collectives: 982 us -> none  [body(): lax.psum(flop_weight[0] * turn_share / lax.axis_size('board'), 'board')]
    pmax x1 -> x0, waiting for transfers between devices: 151 us -> none  [node_part(): merged = lax.pmax(buffer, 'seq')]
    pallas_call x0 -> x3, Pallas kernels: none -> 74.1 us  [the longest x1 56.1 us: reduce(): pl.pallas_call(reduce_kernel, name='exchange_reduce', out_shape=(jax.Shap...]
  transfers between devices with their start and end apart: 1 -> 0, of which waited for: 1 -> 0; matrix products, arithmetic and copies ran while one was open for 0% -> 0% of each run, Pallas kernels for 0% -> 0%
where the time goes in v1:
time: 86.9 us; the launch traced here: 86.2 us
  Pallas kernels  74.1 us (85%)
  local copies, waits for them, and re-layouts  10.2 us (12%)
  between operations  1.98 us (2%)
    pallas_call x1, Pallas kernels, reduce(): pl.pallas_call(reduce_kernel, name='exchange_reduce', out_shape=(jax.Shap...  56.1 us
    pallas_call x1, Pallas kernels, compute(): pl.pallas_call(compute_kernel, name='river_maxima', out_shape=jax.ShapeDt...  9.84 us
    unnamed x16, local copies, waits for them, and re-layouts  9.42 us
    pallas_call x1, Pallas kernels, gather(): pl.pallas_call(gather_kernel, name='gather_reach', out_shape=jax.ShapeDty...  8.1 us

profile of v1, /device:TPU:1, one launch (start us, length us, event | category | flops | bytes accessed | tf_op | source)
XLA Modules:
  0.0 86.2 jit_solution(12223020450709184742)
XLA Ops:
  0.6 8.1 %gather_reach.1.reach_ref = f32[24,1326]{1,0:T(8,128)} custom-call(bf16[1,6,1326]{2,1,0:T(8,128)(2,1)} %reach_ref.1), custom_call_target="tpu_custom_call" | custom-call | tf_op jit(solution)/shard_map/gather_reach/pallas_call | solution.py:73
  8.7 0.8 copy.16
  9.5 0.7 copy.12.pacol_ref
  10.3 0.8 copy.11
  11.7 0.0 copy-start.1
  11.7 1.1 %copy-done.1 = bf16[1,6,48,1326]{3,2,1,0:T(8,128)(2,1)S(1)} copy-done((bf16[1,6,48,1326]{3,2,1,0:T(8,128)(2,1)S(1)}, bf16[1,6,48,1326]{3,2,1,0:T(8,128)(2,1)}, u32[]{:S(2)}) %copy-start.1) | copy-done | bytes 763800
  12.8 0.0 copy-start.2
  12.8 0.9 %copy-done.2 = f32[24,1326]{1,0:T(8,128)S(1)} copy-done((f32[24,1326]{1,0:T(8,128)S(1)}, f32[24,1326]{1,0:T(8,128)}, u32[]{:S(2)}) %copy-start.2) | copy-done | bytes 127320
  13.7 0.0 copy-start.3
  13.7 0.7 copy-done.3
  14.4 0.0 copy-start.4
  14.4 0.7 copy-done.4
  15.1 0.0 copy-start.5
  15.1 0.7 copy-done.5
  15.7 9.8 %river_maxima.1.part_ref = f32[4,6,6,1326]{3,2,1,0:T(8,128)S(1)} custom-call(s32[6,5]{1,0:T(8,128)S(1)} %bitcast.11, s32[6,1326]{1,0:T(8,128)S(1)} %bitcast.10, s32[1]{0:T(128)S(6)} %copy.18.count_ref, f32[24,1326]{1,0:T(8,128)S(1)} %copy-done.2, bf16[6,48,1326]{2,1,0:T(8,128)(2,1)S(1)} %bitcast.9, s32[1,48]{1,0:T(1,128)S(1)} %bitcast.13, ...), custom_call_target="tpu_custom_call" | custom-call | tf_op jit(solution)/shard_map/river_maxima/pallas_call | solution.py:167
  25.6 0.0 copy-start
  25.6 1.0 %copy-done = f32[4,6,6,1326]{3,2,1,0:T(8,128)} copy-done((f32[4,6,6,1326]{3,2,1,0:T(8,128)}, f32[4,6,6,1326]{3,2,1,0:T(8,128)S(1)}, u32[]{:S(2)}) %copy-start) | copy-done | bytes 763800
  27.2 56.1 %exchange_reduce.1 = (f32[6,1326]{1,0:T(8,128)}, f32[6,1326]{1,0:T(8,128)}) custom-call(f32[4,6,6,1326]{3,2,1,0:T(8,128)} %copy-done, f32[1]{0:T(128)S(6)} %copy.19.weight_ref), custom_call_target="tpu_custom_call" | custom-call | tf_op jit(solution)/shard_map/exchange_reduce/pallas_call | solution.py:239
  83.4 1.4 %copy.13 = f32[1,6,1326]{2,0,1:T(1,128)} copy(f32[1,6,1326]{2,1,0:T(8,128)} %bitcast.15) | data formatting | bytes 63648
  84.8 1.4 %copy.20 = f32[6,1326]{1,0:T(8,128)} copy(f32[6,1326]{1,0:T(8,128)} %get-tuple-element.11) | data formatting | bytes 63648
Async XLA Ops:
  11.7 1.1 %copy-start.1 = (bf16[1,6,48,1326]{3,2,1,0:T(8,128)(2,1)S(1)}, bf16[1,6,48,1326]{3,2,1,0:T(8,128)(2,1)}, u32[]{:S(2)}) copy-start(bf16[1,6,48,1326]{3,2,1,0:T(8,128)(2,1)} %param.13) | copy-start | bytes 2291332
  12.8 0.9 %copy-start.2 = (f32[24,1326]{1,0:T(8,128)S(1)}, f32[24,1326]{1,0:T(8,128)}, u32[]{:S(2)}) copy-start(f32[24,1326]{1,0:T(8,128)} %gather_reach.1.reach_ref) | copy-start | bytes 381892
  13.7 0.7 copy-start.3
  14.4 0.7 copy-start.4
  15.1 0.7 copy-start.5
  25.6 1.0 %copy-start = (f32[4,6,6,1326]{3,2,1,0:T(8,128)}, f32[4,6,6,1326]{3,2,1,0:T(8,128)S(1)}, u32[]{:S(2)}) copy-start(f32[4,6,6,1326]{3,2,1,0:T(8,128)S(1)} %river_maxima.1.part_ref) | copy-start | bytes 2291332

commit v2 on v1

v2 whole, which is shorter than its diff:
```python
import jax
import jax.numpy as jnp
import numpy as np
from jax import lax
from jax.experimental import pallas as pl
from jax.experimental.pallas import tpu as pltpu
from jax.sharding import PartitionSpec as P

HANDS, NODES, RIVERS, LEAF = 1326, 24, 6, 48
NX, NY, NZ, NC = 4, 8, 16, 2
GROUP = NY * NC
SLOTS = 8 * NODES
PART = NODES // NX
TILES = -(-HANDS // 128)
lowest = -1000000000.0
MESH = pl.DeviceIdType.MESH
VM = pl.BlockSpec(memory_space=pltpu.VMEM)
HBM = pl.BlockSpec(memory_space=pl.ANY)
SM = pl.BlockSpec(memory_space=pltpu.SMEM)
f32, bf16 = jnp.float32, jnp.bfloat16


def seq_peer(d):
    return (lax.axis_index("board"), lax.rem(lax.axis_index("seq") + d, NX))


def place():
    board = lax.axis_index("board")
    core = lax.rem(board, NC)
    z = lax.rem(board // NC, NZ)
    return board // (NC * NZ), z, core


def group_peer(d):
    y, z, core = place()
    g = lax.rem(y * NC + core + d, GROUP)
    return ((g // NC * NZ + z) * NC + lax.rem(g, NC), lax.axis_index("seq"))


def line_peer(d):
    y, z, core = place()
    return ((y * NZ + lax.rem(z + d, NZ)) * NC + core, lax.axis_index("seq"))


def meet(peers):
    barrier = pltpu.get_barrier_semaphore()
    for peer in peers:
        pl.semaphore_signal(barrier, inc=1, device_id=peer, device_id_type=MESH)
    pl.semaphore_wait(barrier, len(peers))


def send(src, dst, send_sem, recv_sem, peer):
    copy = pltpu.make_async_remote_copy(
        src_ref=src, dst_ref=dst, send_sem=send_sem, recv_sem=recv_sem, device_id=peer, device_id_type=MESH
    )
    copy.start()
    return copy


CHUNK = 256


def far_first(n, width=1):
    return sorted(range(1, n), key=lambda d: -min(d // width, n // width - d // width))


def prepare(tab_ref, mask_ref, rank_ref, row_ref, col_ref, colb_ref, cards_ref, count_ref, scale_ref):
    low = tab_ref[0:1, :]
    high = tab_ref[1:2, :]
    card = lax.broadcasted_iota(jnp.int32, (64, HANDS), 0)
    onehot = jnp.where((card == low) | (card == high), 1.0, 0.0).astype(bf16)
    for j in range(0, HANDS, CHUNK):
        w = min(CHUNK, HANDS - j)
        shared = lax.dot_general(
            onehot, onehot[:, j : j + w], (((0,), (0,)), ((), ())), preferred_element_type=f32
        )
        mask_ref[:, j : j + w] = (1.0 - jnp.minimum(shared, 1.0)).astype(bf16)
    count = jnp.full((1, HANDS), count_ref[0], jnp.int32)
    share = 1.0 / (HANDS * count.astype(f32))
    for r in range(RIVERS):
        row_ref[r : r + 1, :] = rank_ref[r].astype(f32)
        hit = jnp.zeros((1, HANDS), jnp.bool_)
        for i in range(5):
            hit = hit | (low == cards_ref[i, 0, r]) | (high == cards_ref[i, 0, r])
        live = jnp.where(hit, 0.0, 1.0)
        scale_ref[r : r + 1, :] = live
        scale_ref[8 + r : 9 + r, :] = live * jnp.where(count > r, share, 0.0)
    col_ref[...] = row_ref[...].T
    for r in range(RIVERS):
        colb_ref[r] = jnp.broadcast_to(col_ref[:, r : r + 1], (HANDS, 128))


def place_leaves(parent_ref, pot_ref, oh_ref, potb_ref, biasb_ref):
    prow = parent_ref[...]
    si = lax.broadcasted_iota(jnp.int32, (LEAF, LEAF), 0)
    sj = lax.broadcasted_iota(jnp.int32, (LEAF, LEAF), 1)
    pcol = jnp.sum(jnp.where(si == sj, prow.astype(f32), 0.0), axis=1, keepdims=True).astype(jnp.int32)
    before = jnp.sum(jnp.where((prow == pcol) & (si < sj), 1.0, 0.0), axis=0, keepdims=True).astype(jnp.int32)
    oh = lax.broadcasted_iota(jnp.int32, (SLOTS, LEAF), 0) == before * NODES + prow
    oh_ref[...] = jnp.where(oh, 1.0, 0.0).astype(bf16)
    pot = jnp.sum(jnp.where(oh, pot_ref[...], 0.0), axis=1, keepdims=True)
    used = jnp.sum(jnp.where(oh, 1.0, 0.0), axis=1, keepdims=True)
    potb_ref[...] = jnp.broadcast_to(pot, (SLOTS, 128))
    biasb_ref[...] = jnp.broadcast_to(jnp.where(used > 0.5, 0.0, lowest), (SLOTS, 128))


def payoff(r, j, w, row_ref, colb_ref, mask_ref):
    col = jnp.concatenate([colb_ref[r]] * (CHUNK // 128), axis=1)
    gap = row_ref[r : r + 1, j : j + w] - col[:, :w]
    return jnp.clip(gap, -1.0, 1.0).astype(bf16) * mask_ref[:, j : j + w]


def river_kernel(
    cards_ref, count_ref, weight_ref, rank_hbm, reach_hbm, strat_hbm, parent_hbm, pot_hbm, tab_hbm,
    turn_ref, root_ref,
    rank_ref, reach_ref, strat_ref, parent_ref, pot_ref, tab_ref,
    mask_ref, row_ref, col_ref, colb_ref, scale_ref, oh_ref, potb_ref, biasb_ref,
    part_ref, relay_ref, comb_ref, back_ref, ahead_ref, last_ref,
    mine_ref, in1_ref, sum1_ref, in2_ref, sum2_ref, in3_ref,
    local, sg, rg, sa, ra, sb, rb, sc, rc, sl, rl, s1, r1, s2, r2, s3, r3,
):
    x = lax.axis_index("seq")
    y, z, core = place()
    g = y * NC + core
    group_order = far_first(GROUP, NC)
    line_order = far_first(NZ)
    pairs = [(tab_hbm, tab_ref), (rank_hbm, rank_ref), (parent_hbm, parent_ref), (pot_hbm, pot_ref),
             (reach_hbm.at[0], reach_ref.at[x]), (strat_hbm.at[0], strat_ref)]
    fetch = [pltpu.make_async_copy(a, b, local.at[i]) for i, (a, b) in enumerate(pairs)]
    for copy in fetch:
        copy.start()
    peers = [line_peer(d) for d in line_order] + [group_peer(d) for d in group_order]
    peers += [seq_peer(d) for d in (2, 1, 3)]
    barrier = pltpu.get_barrier_semaphore()
    for peer in peers:
        pl.semaphore_signal(barrier, inc=1, device_id=peer, device_id_type=MESH)
    for copy in fetch[:4]:
        copy.wait()
    place_leaves(parent_ref, pot_ref, oh_ref, potb_ref, biasb_ref)
    mine_ref[...] = jnp.zeros_like(mine_ref)
    prepare(tab_ref, mask_ref, rank_ref, row_ref, col_ref, colb_ref, cards_ref, count_ref, scale_ref)
    pl.semaphore_wait(barrier, len(peers))

    copies = [
        send(reach_hbm.at[0], reach_ref.at[x], sg.at[d], rg.at[d], seq_peer(d)) for d in (2, 1, 3)
    ]
    for copy in fetch[4:]:
        copy.wait()
    for copy in copies:
        copy.wait()
    reach = jnp.concatenate([reach_ref[i].astype(f32) for i in range(NX)], axis=0)
    pot2 = jnp.concatenate([potb_ref[...]] * (CHUNK // 128), axis=1)
    bias2 = jnp.concatenate([biasb_ref[...]] * (CHUNK // 128), axis=1)

    def river(r):
        leaf = jnp.dot(oh_ref[...], strat_ref[r], preferred_element_type=f32).reshape(8, NODES, HANDS)
        leaf = (leaf * (reach * scale_ref[r : r + 1, :])[None]).reshape(SLOTS, HANDS).astype(bf16)
        for j in range(0, HANDS, CHUNK):
            w = min(CHUNK, HANDS - j)
            pay = payoff(r, j, w, row_ref, colb_ref, mask_ref)
            val = jnp.dot(leaf, pay, preferred_element_type=f32)
            val = (val * pot2[:, :w] + bias2[:, :w]).reshape(8, NODES, w)
            best = jnp.max(val, axis=0) * scale_ref[8 + r : 9 + r, j : j + w]
            for i in range(NX):
                part_ref[i, r, :, j : j + w] = best[PART * i : PART * (i + 1)]

    def step(r):
        return (1, NX - 1) if r % 2 == 0 else (NX - 1, 1)

    first, direct, second = {}, {}, {}

    def combine(r):
        ahead, behind = step(r)
        first[r].wait_recv()
        comb_ref[r] = jnp.maximum(part_ref[lax.rem(x + ahead, NX), r], relay_ref[r])
        second[r] = send(comb_ref.at[r], ahead_ref.at[r], sc.at[r], rc.at[r], seq_peer(ahead))

    def collect(r):
        direct[r].wait_recv()
        second[r].wait_recv()
        return jnp.maximum(part_ref[x, r], jnp.maximum(back_ref[r], ahead_ref[r]))

    total = jnp.zeros((PART, HANDS), f32)
    end = RIVERS - 1
    for r in range(RIVERS):
        river(r)
        if r < end:
            ahead, behind = step(r)
            first[r] = send(
                part_ref.at[lax.rem(x + 2, NX), r], relay_ref.at[r], sa.at[r], ra.at[r], seq_peer(ahead)
            )
            direct[r] = send(
                part_ref.at[lax.rem(x + behind, NX), r], back_ref.at[r], sb.at[r], rb.at[r], seq_peer(behind)
            )
        else:
            copies = [
                send(part_ref.at[lax.rem(x + d, NX), r], last_ref.at[d - 1], sl.at[d - 1], rl.at[d - 1], seq_peer(d))
                for d in (2, 1, 3)
            ]
        if r >= 1:
            combine(r - 1)
        if r >= 2:
            total = total + collect(r - 2)
    total = total + collect(end - 1)
    for copy in copies:
        copy.wait_recv()
    best = jnp.maximum(part_ref[x, end], jnp.maximum(last_ref[0], jnp.maximum(last_ref[1], last_ref[2])))
    turn = total + best
    share = turn * (weight_ref[0] / (NY * NZ * NC))
    for j in range(TILES):
        w = min(128, HANDS - 128 * j)
        mine_ref[j, 0:PART, 0:w] = share[:, 128 * j : 128 * j + w]
    copies1 = {
        d: send(mine_ref.at[lax.rem(g + d, GROUP)], in1_ref.at[d], s1.at[d], r1.at[d], group_peer(d))
        for d in group_order
    }
    turn_ref[...] = turn
    for d in reversed(group_order):
        copies1[d].wait_recv()
    in1_ref[0] = mine_ref[g]
    part1 = jnp.sum(in1_ref[...], axis=0)
    sum1_ref[...] = part1
    copies2 = [send(sum1_ref, in2_ref.at[z], s2.at[d], r2.at[d], line_peer(d)) for d in line_order]
    in2_ref[z] = part1
    for copy in reversed(copies2):
        copy.wait_recv()
    part2 = jnp.sum(in2_ref[...], axis=0)
    sum2_ref[...] = part2
    copies3 = [send(sum2_ref, in3_ref.at[g], s3.at[d], r3.at[d], group_peer(d)) for d in group_order]
    in3_ref[g] = part2
    for copy in copies:
        copy.wait_send()
    for r in range(end):
        first[r].wait_send()
        direct[r].wait_send()
        second[r].wait_send()
    for copy in list(copies1.values()) + copies2:
        copy.wait_send()
    for copy in reversed(copies3):
        copy.wait()
    for j in range(TILES):
        w = min(128, HANDS - 128 * j)
        root_ref[:, 128 * j : 128 * j + w] = in3_ref[j, 0:PART, 0:w]


def body(
    board_cards, hand_ranks, river_count, reach_in, strategy, parent_node, pot_size, flop_weight
):
    tab = jnp.asarray(np.stack(np.triu_indices(52, 1)), jnp.int32)
    slab = (PART, HANDS)
    tile = (8, 128)
    vm, dma = pltpu.VMEM, pltpu.SemaphoreType.DMA
    scratch = [
        vm((RIVERS, 1, HANDS), jnp.int32),
        vm((NX, PART, HANDS), bf16),
        vm((RIVERS, LEAF, HANDS), bf16),
        vm((1, LEAF), jnp.int32),
        vm((1, LEAF), f32),
        vm((2, HANDS), jnp.int32),
        vm((HANDS, HANDS), bf16),
        vm((8, HANDS), f32),
        vm((HANDS, 8), f32),
        vm((RIVERS, HANDS, 128), f32),
        vm((16, HANDS), f32),
        vm((SLOTS, LEAF), bf16),
        vm((SLOTS, 128), f32),
        vm((SLOTS, 128), f32),
        vm((NX, RIVERS) + slab, f32),
        vm((RIVERS,) + slab, f32),
        vm((RIVERS,) + slab, f32),
        vm((RIVERS,) + slab, f32),
        vm((RIVERS,) + slab, f32),
        vm((NX - 1,) + slab, f32),
        vm((GROUP,) + tile, f32),
        vm((GROUP,) + tile, f32),
        vm(tile, f32),
        vm((NZ,) + tile, f32),
        vm(tile, f32),
        vm((GROUP,) + tile, f32),
    ]
    sems = (6, NX, NX) + (RIVERS,) * 6 + (NX, NX, GROUP, GROUP, NZ, NZ, GROUP, GROUP)
    turn, root = pl.pallas_call(
        river_kernel,
        name="river_values",
        out_shape=(jax.ShapeDtypeStruct(slab, f32), jax.ShapeDtypeStruct(slab, f32)),
        in_specs=[SM, SM, SM] + [HBM] * 6,
        out_specs=(VM, VM),
        scratch_shapes=scratch + [dma((n,)) for n in sems],
        compiler_params=pltpu.CompilerParams(
            collective_id=0, has_side_effects=True, vmem_limit_bytes=60 << 20
        ),
    )(
        jnp.transpose(board_cards, (2, 0, 1)),
        river_count,
        flop_weight,
        jnp.transpose(hand_ranks, (1, 0, 2)),
        reach_in,
        strategy,
        parent_node[None, :],
        pot_size[None, :],
        tab,
    )
    return (turn[None], root)


def solution(mesh):
    return jax.shard_map(
        body,
        mesh=mesh,
        in_specs=(
            P("board", None, None),
            P("board", None, None),
            P("board"),
            P("board", "seq", None),
            P("board", None, "seq", None),
            P("seq"),
            P("seq"),
            P("board"),
        ),
        out_specs=(P("board", "seq", None), P("seq", None)),
        check_vma=False,
    )
```

time: 86.9 us -> 70.5 us (0.81)
  local copies, waits for them, and re-layouts: 10.2 us -> 2.07 us
  Pallas kernels: 74.1 us -> 66.2 us
    pallas_call x3 -> x1, Pallas kernels: 74.1 us -> 66.2 us  [body(): pl.pallas_call(river_kernel, name='river_values', out_shape=(jax.ShapeDty...]
    unnamed x16 -> x4, local copies, waits for them, and re-layouts: 9.42 us -> 2.07 us
where the time goes in v2:
time: 70.5 us; the launch traced here: 70.2 us
  Pallas kernels  66.2 us (94%)
  local copies, waits for them, and re-layouts  2.07 us (3%)
  between operations  1.94 us (3%)
    pallas_call x1, Pallas kernels, body(): pl.pallas_call(river_kernel, name='river_values', out_shape=(jax.ShapeDty...  66.2 us
    unnamed x4, local copies, waits for them, and re-layouts  2.07 us

profile of v2, /device:TPU:1, one launch (start us, length us, event | category | flops | bytes accessed | tf_op | source)
XLA Modules:
  0.0 70.2 jit_solution(4089031096157677495)
XLA Ops:
  1.9 66.2 %river_values.1 = (f32[6,1326]{1,0:T(8,128)}, f32[6,1326]{1,0:T(8,128)}) custom-call(s32[5,1,6]{2,1,0:T(1,128)} %bitcast.7, s32[1]{0:T(128)S(6)} %copy.13.count_ref, f32[1]{0:T(128)S(6)} %copy.14.weight_ref, s32[6,1,1326]{2,1,0:T(1,128)} %bitcast.6, bf16[1,6,1326]{2,1,0:T(8,128)(2,1)} %reach_hbm.1, bf16[1,6,48,1326]{3,2,1,0:T(8,128)(2,1)} %strat_hbm.1, ...), custom_call_target="tpu_custom_call" | custom-call | tf_op jit(solution)/shard_map/river_values/pallas_call | solution.py:282
  68.2 0.0 copy-start
  68.2 1.4 %copy.11 = f32[1,6,1326]{2,0,1:T(1,128)} copy(f32[1,6,1326]{2,1,0:T(8,128)} %bitcast.5) | data formatting | bytes 63648
  69.6 0.0 copy-done
  69.6 0.6 copy.15
Async XLA Ops:
  68.2 1.5 %copy-start = (f32[6,1326]{1,0:T(8,128)S(1)}, f32[6,1326]{1,0:T(8,128)}, u32[]{:S(2)}) copy-start(f32[6,1326]{1,0:T(8,128)} %get-tuple-element.11) | copy-start | bytes 95476

commit v3 on v2

--- a/solution.py
+++ b/solution.py
@@ -42,17 +42,14 @@
     return ((y * NZ + lax.rem(z + d, NZ)) * NC + core, lax.axis_index("seq"))
 
 
-def meet(peers):
-    barrier = pltpu.get_barrier_semaphore()
-    for peer in peers:
-        pl.semaphore_signal(barrier, inc=1, device_id=peer, device_id_type=MESH)
-    pl.semaphore_wait(barrier, len(peers))
-
-
-def send(src, dst, send_sem, recv_sem, peer):
-    copy = pltpu.make_async_remote_copy(
+def move(src, dst, send_sem, recv_sem, peer):
+    return pltpu.make_async_remote_copy(
         src_ref=src, dst_ref=dst, send_sem=send_sem, recv_sem=recv_sem, device_id=peer, device_id_type=MESH
     )
+
+
+def send(*args):
+    copy = move(*args)
     copy.start()
     return copy
 
@@ -117,7 +114,7 @@
     mask_ref, row_ref, col_ref, colb_ref, scale_ref, oh_ref, potb_ref, biasb_ref,
     part_ref, relay_ref, comb_ref, back_ref, ahead_ref, last_ref,
     mine_ref, in1_ref, sum1_ref, in2_ref, sum2_ref, in3_ref,
-    local, sg, rg, sa, ra, sb, rb, sc, rc, sl, rl, s1, r1, s2, r2, s3, r3,
+    known_y, known_z, known_far, local, sg, rg, sa, ra, sb, rb, sc, rc, sl, rl, s1, r1, s2, r2, s3, r3,
 ):
     x = lax.axis_index("seq")
     y, z, core = place()
@@ -129,7 +126,8 @@
     fetch = [pltpu.make_async_copy(a, b, local.at[i]) for i, (a, b) in enumerate(pairs)]
     for copy in fetch:
         copy.start()
-    peers = [line_peer(d) for d in line_order] + [group_peer(d) for d in group_order]
+    near = [d for d in group_order if abs(d - GROUP * (d > GROUP // 2)) // NC <= 2]
+    peers = [line_peer(d) for d in (2, NZ - 2, 1, NZ - 1)] + [group_peer(d) for d in near]
     peers += [seq_peer(d) for d in (2, 1, 3)]
     barrier = pltpu.get_barrier_semaphore()
     for peer in peers:
@@ -137,13 +135,15 @@
     for copy in fetch[:4]:
         copy.wait()
     place_leaves(parent_ref, pot_ref, oh_ref, potb_ref, biasb_ref)
-    mine_ref[...] = jnp.zeros_like(mine_ref)
-    prepare(tab_ref, mask_ref, rank_ref, row_ref, col_ref, colb_ref, cards_ref, count_ref, scale_ref)
     pl.semaphore_wait(barrier, len(peers))
-
     copies = [
         send(reach_hbm.at[0], reach_ref.at[x], sg.at[d], rg.at[d], seq_peer(d)) for d in (2, 1, 3)
     ]
+    for sem, peer in ((known_y, group_peer(2 * NC)), (known_y, group_peer(GROUP - 2 * NC)),
+                      (known_z, line_peer(2)), (known_z, line_peer(NZ - 2))):
+        pl.semaphore_signal(sem, inc=1, device_id=peer, device_id_type=MESH)
+    prepare(tab_ref, mask_ref, rank_ref, row_ref, col_ref, colb_ref, cards_ref, count_ref, scale_ref)
+    mine_ref[...] = jnp.zeros_like(mine_ref)
     for copy in fetch[4:]:
         copy.wait()
     for copy in copies:
@@ -165,7 +165,7 @@
                 part_ref[i, r, :, j : j + w] = best[PART * i : PART * (i + 1)]
 
     def step(r):
-        return (1, NX - 1) if r % 2 == 0 else (NX - 1, 1)
+        return (NX - 1, 1) if r % 2 == 0 else (1, NX - 1)
 
     first, direct, second = {}, {}, {}
 
@@ -184,6 +184,13 @@
     end = RIVERS - 1
     for r in range(RIVERS):
         river(r)
+        if r == 1:
+            pl.semaphore_wait(known_y, 2)
+            pl.semaphore_wait(known_z, 2)
+            for peer in (line_peer(4), line_peer(NZ - 4)):
+                pl.semaphore_signal(known_far, inc=1, device_id=peer, device_id_type=MESH)
+        if r == 4:
+            pl.semaphore_wait(known_far, 2)
         if r < end:
             ahead, behind = step(r)
             first[r] = send(
@@ -197,11 +204,13 @@
                 send(part_ref.at[lax.rem(x + d, NX), r], last_ref.at[d - 1], sl.at[d - 1], rl.at[d - 1], seq_peer(d))
                 for d in (2, 1, 3)
             ]
-        if r >= 1:
-            combine(r - 1)
         if r >= 2:
-            total = total + collect(r - 2)
-    total = total + collect(end - 1)
+            combine(r - 2)
+        if r >= 4:
+            total = total + collect(r - 4)
+    combine(end - 1)
+    for r in range(end - 3, end):
+        total = total + collect(r)
     for copy in copies:
         copy.wait_recv()
     best = jnp.maximum(part_ref[x, end], jnp.maximum(last_ref[0], jnp.maximum(last_ref[1], last_ref[2])))
@@ -209,38 +218,56 @@
     share = turn * (weight_ref[0] / (NY * NZ * NC))
     for j in range(TILES):
         w = min(128, HANDS - 128 * j)
-        mine_ref[j, 0:PART, 0:w] = share[:, 128 * j : 128 * j + w]
+        mine_ref[j, :, 0:w] = share[:, 128 * j : 128 * j + w]
+
+    def other(d):
+        return lax.rem(g + d, GROUP)
+
     copies1 = {
-        d: send(mine_ref.at[lax.rem(g + d, GROUP)], in1_ref.at[d], s1.at[d], r1.at[d], group_peer(d))
-        for d in group_order
+        d: move(mine_ref.at[other(d)], in1_ref.at[d], s1.at[d], r1.at[d], group_peer(d)) for d in group_order
     }
-    turn_ref[...] = turn
-    for d in reversed(group_order):
-        copies1[d].wait_recv()
-    in1_ref[0] = mine_ref[g]
-    part1 = jnp.sum(in1_ref[...], axis=0)
-    sum1_ref[...] = part1
-    copies2 = [send(sum1_ref, in2_ref.at[z], s2.at[d], r2.at[d], line_peer(d)) for d in line_order]
-    in2_ref[z] = part1
-    for copy in reversed(copies2):
-        copy.wait_recv()
-    part2 = jnp.sum(in2_ref[...], axis=0)
-    sum2_ref[...] = part2
-    copies3 = [send(sum2_ref, in3_ref.at[g], s3.at[d], r3.at[d], group_peer(d)) for d in group_order]
-    in3_ref[g] = part2
+    copies2 = [move(sum1_ref, in2_ref.at[z], s2.at[d], r2.at[d], line_peer(d)) for d in line_order]
+    copies3 = {d: move(sum2_ref, in3_ref.at[g], s3.at[d], r3.at[d], group_peer(d)) for d in group_order}
+    for d in group_order:
+        pl.when(other(d) < TILES)(copies1[d].start)
+    for i in range(PART):
+        turn_ref[i] = turn[i : i + 1]
+
+    @pl.when(g < TILES)
+    def _():
+        in1_ref[0] = mine_ref[g]
+        for d in reversed(group_order):
+            copies1[d].wait_recv()
+        part1 = jnp.sum(in1_ref[...], axis=0)
+        sum1_ref[...] = part1
+        for copy in copies2:
+            copy.start()
+        in2_ref[z] = part1
+        for copy in reversed(copies2):
+            copy.wait_recv()
+        part2 = jnp.sum(in2_ref[...], axis=0)
+        sum2_ref[...] = part2
+        for d in group_order:
+            copies3[d].start()
+        in3_ref[g] = part2
+        for copy in copies2:
+            copy.wait_send()
+        for d in group_order:
+            copies3[d].wait_send()
+
     for copy in copies:
         copy.wait_send()
     for r in range(end):
         first[r].wait_send()
         direct[r].wait_send()
         second[r].wait_send()
-    for copy in list(copies1.values()) + copies2:
-        copy.wait_send()
-    for copy in reversed(copies3):
-        copy.wait()
+    for d in group_order:
+        pl.when(other(d) < TILES)(copies1[d].wait_send)
+    for d in reversed(group_order):
+        pl.when(other(GROUP - d) < TILES)(copies3[d].wait_recv)
     for j in range(TILES):
         w = min(128, HANDS - 128 * j)
-        root_ref[:, 128 * j : 128 * j + w] = in3_ref[j, 0:PART, 0:w]
+        root_ref[:, 128 * j : 128 * j + w] = in3_ref[j, :, 0:w]
 
 
 def body(
@@ -248,7 +275,7 @@
 ):
     tab = jnp.asarray(np.stack(np.triu_indices(52, 1)), jnp.int32)
     slab = (PART, HANDS)
-    tile = (8, 128)
+    tile = (PART, 128)
     vm, dma = pltpu.VMEM, pltpu.SemaphoreType.DMA
     scratch = [
         vm((RIVERS, 1, HANDS), jnp.int32),
@@ -282,10 +309,10 @@
     turn, root = pl.pallas_call(
         river_kernel,
         name="river_values",
-        out_shape=(jax.ShapeDtypeStruct(slab, f32), jax.ShapeDtypeStruct(slab, f32)),
+        out_shape=(jax.ShapeDtypeStruct((PART, 1, HANDS), f32), jax.ShapeDtypeStruct(slab, f32)),
         in_specs=[SM, SM, SM] + [HBM] * 6,
         out_specs=(VM, VM),
-        scratch_shapes=scratch + [dma((n,)) for n in sems],
+        scratch_shapes=scratch + [pltpu.SemaphoreType.REGULAR] * 3 + [dma((n,)) for n in sems],
         compiler_params=pltpu.CompilerParams(
             collective_id=0, has_side_effects=True, vmem_limit_bytes=60 << 20
         ),
@@ -300,7 +327,7 @@
         pot_size[None, :],
         tab,
     )
-    return (turn[None], root)
+    return (jnp.transpose(turn, (1, 0, 2)), root)
 
 
 def solution(mesh):

time: 70.5 us -> 62.5 us (0.89)
  Pallas kernels: 66.2 us -> 58.2 us
    pallas_call x1, Pallas kernels: 66.2 us -> 58.2 us  [body(): pl.pallas_call(river_kernel, name='river_values', out_shape=(jax.ShapeDty...]
where the time goes in v3:
time: 62.5 us; the launch traced here: 62.2 us
  Pallas kernels  58.2 us (93%)
  local copies, waits for them, and re-layouts  2.02 us (3%)
  between operations  1.94 us (3%)
    pallas_call x1, Pallas kernels, body(): pl.pallas_call(river_kernel, name='river_values', out_shape=(jax.ShapeDty...  58.2 us
    unnamed x4, local copies, waits for them, and re-layouts  2.02 us

profile of v3, /device:TPU:1, one launch (start us, length us, event | category | flops | bytes accessed | tf_op | source)
XLA Modules:
  0.0 62.2 jit_solution(12766030435222624348)
XLA Ops:
  1.9 58.2 %river_values.1 = (f32[6,1,1326]{2,1,0:T(1,128)}, f32[6,1326]{1,0:T(8,128)}) custom-call(s32[5,1,6]{2,1,0:T(1,128)} %bitcast.7, s32[1]{0:T(128)S(6)} %copy.13.count_ref, f32[1]{0:T(128)S(6)} %copy.14.weight_ref, s32[6,1,1326]{2,1,0:T(1,128)} %bitcast.5, bf16[1,6,1326]{2,1,0:T(8,128)(2,1)} %reach_hbm.1, bf16[1,6,48,1326]{3,2,1,0:T(8,128)(2,1)} %strat_hbm.1, ...), custom_call_target="tpu_custom_call" | custom-call | tf_op jit(solution)/shard_map/river_values/pallas_call | solution.py:309
  60.2 0.0 copy-start
  60.2 1.4 %copy.15 = f32[1,6,1326]{2,0,1:T(1,128)} copy(f32[1,6,1326]{2,0,1:T(1,128)} %bitcast.6) | data formatting | bytes 63648
  61.6 0.0 copy-done
  61.6 0.6 copy.16
Async XLA Ops:
  60.2 1.4 %copy-start = (f32[6,1326]{1,0:T(8,128)S(1)}, f32[6,1326]{1,0:T(8,128)}, u32[]{:S(2)}) copy-start(f32[6,1326]{1,0:T(8,128)} %get-tuple-element.9) | copy-start | bytes 95476

commit v4 on v3

--- a/solution.py
+++ b/solution.py
@@ -11,7 +11,9 @@
 GROUP = NY * NC
 SLOTS = 8 * NODES
 PART = NODES // NX
-TILES = -(-HANDS // 128)
+WIDE = 1152
+REST = HANDS - WIDE
+TILES = WIDE // 128
 lowest = -1000000000.0
 MESH = pl.DeviceIdType.MESH
 VM = pl.BlockSpec(memory_space=pltpu.VMEM)
@@ -55,6 +57,7 @@
 
 
 CHUNK = 256
+CHUNKS = [(j, CHUNK) for j in range(0, 1024, CHUNK)] + [(1024, 128), (WIDE, REST)]
 
 
 def far_first(n, width=1):
@@ -101,6 +104,10 @@
     biasb_ref[...] = jnp.broadcast_to(jnp.where(used > 0.5, 0.0, lowest), (SLOTS, 128))
 
 
+def spare(i):
+    return PART + i // 4, i % 4 * 256
+
+
 def payoff(r, j, w, row_ref, colb_ref, mask_ref):
     col = jnp.concatenate([colb_ref[r]] * (CHUNK // 128), axis=1)
     gap = row_ref[r : r + 1, j : j + w] - col[:, :w]
@@ -108,10 +115,10 @@
 
 
 def river_kernel(
-    cards_ref, count_ref, weight_ref, rank_hbm, reach_hbm, strat_hbm, parent_hbm, pot_hbm, tab_hbm,
+    cards_hbm, count_ref, weight_ref, rank_hbm, reach_hbm, strat_hbm, parent_hbm, pot_hbm, tab_hbm,
     turn_ref, root_ref,
-    rank_ref, reach_ref, strat_ref, parent_ref, pot_ref, tab_ref,
-    mask_ref, row_ref, col_ref, colb_ref, scale_ref, oh_ref, potb_ref, biasb_ref,
+    cards_ref, rank_ref, reach_ref, strat_ref, parent_ref, pot_ref, tab_ref,
+    pay_ref, mask_ref, row_ref, col_ref, colb_ref, scale_ref, oh_ref, potb_ref, biasb_ref,
     part_ref, relay_ref, comb_ref, back_ref, ahead_ref, last_ref,
     mine_ref, in1_ref, sum1_ref, in2_ref, sum2_ref, in3_ref,
     known_y, known_z, known_far, local, sg, rg, sa, ra, sb, rb, sc, rc, sl, rl, s1, r1, s2, r2, s3, r3,
@@ -121,7 +128,7 @@
     g = y * NC + core
     group_order = far_first(GROUP, NC)
     line_order = far_first(NZ)
-    pairs = [(tab_hbm, tab_ref), (rank_hbm, rank_ref), (parent_hbm, parent_ref), (pot_hbm, pot_ref),
+    pairs = [(cards_hbm, cards_ref), (tab_hbm, tab_ref), (rank_hbm, rank_ref), (parent_hbm, parent_ref), (pot_hbm, pot_ref),
              (reach_hbm.at[0], reach_ref.at[x]), (strat_hbm.at[0], strat_ref)]
     fetch = [pltpu.make_async_copy(a, b, local.at[i]) for i, (a, b) in enumerate(pairs)]
     for copy in fetch:
@@ -132,7 +139,7 @@
     barrier = pltpu.get_barrier_semaphore()
     for peer in peers:
         pl.semaphore_signal(barrier, inc=1, device_id=peer, device_id_type=MESH)
-    for copy in fetch[:4]:
+    for copy in fetch[:5]:
         copy.wait()
     place_leaves(parent_ref, pot_ref, oh_ref, potb_ref, biasb_ref)
     pl.semaphore_wait(barrier, len(peers))
@@ -143,8 +150,10 @@
                       (known_z, line_peer(2)), (known_z, line_peer(NZ - 2))):
         pl.semaphore_signal(sem, inc=1, device_id=peer, device_id_type=MESH)
     prepare(tab_ref, mask_ref, rank_ref, row_ref, col_ref, colb_ref, cards_ref, count_ref, scale_ref)
-    mine_ref[...] = jnp.zeros_like(mine_ref)
-    for copy in fetch[4:]:
+    part_ref[:, :, PART:8, :] = jnp.zeros((NX, RIVERS, 8 - PART, WIDE), f32)
+    for j, w in CHUNKS:
+        pay_ref[:, j : j + w] = payoff(0, j, w, row_ref, colb_ref, mask_ref)
+    for copy in fetch[5:]:
         copy.wait()
     for copy in copies:
         copy.wait()
@@ -155,14 +164,21 @@
     def river(r):
         leaf = jnp.dot(oh_ref[...], strat_ref[r], preferred_element_type=f32).reshape(8, NODES, HANDS)
         leaf = (leaf * (reach * scale_ref[r : r + 1, :])[None]).reshape(SLOTS, HANDS).astype(bf16)
-        for j in range(0, HANDS, CHUNK):
-            w = min(CHUNK, HANDS - j)
-            pay = payoff(r, j, w, row_ref, colb_ref, mask_ref)
+        for j, w in CHUNKS:
+            if r == 0:
+                pay = pay_ref[:, j : j + w]
+            else:
+                pay = payoff(r, j, w, row_ref, colb_ref, mask_ref)
             val = jnp.dot(leaf, pay, preferred_element_type=f32)
             val = (val * pot2[:, :w] + bias2[:, :w]).reshape(8, NODES, w)
             best = jnp.max(val, axis=0) * scale_ref[8 + r : 9 + r, j : j + w]
             for i in range(NX):
-                part_ref[i, r, :, j : j + w] = best[PART * i : PART * (i + 1)]
+                if j < WIDE:
+                    part_ref[i, r, 0:PART, j : j + w] = best[PART * i : PART * (i + 1)]
+                else:
+                    for k in range(PART):
+                        row, at = spare(k)
+                        part_ref[i, r, row : row + 1, at : at + w] = best[PART * i + k : PART * i + k + 1]
 
     def step(r):
         return (NX - 1, 1) if r % 2 == 0 else (1, NX - 1)
@@ -180,7 +196,7 @@
         second[r].wait_recv()
         return jnp.maximum(part_ref[x, r], jnp.maximum(back_ref[r], ahead_ref[r]))
 
-    total = jnp.zeros((PART, HANDS), f32)
+    total = jnp.zeros((8, WIDE), f32)
     end = RIVERS - 1
     for r in range(RIVERS):
         river(r)
@@ -217,8 +233,7 @@
     turn = total + best
     share = turn * (weight_ref[0] / (NY * NZ * NC))
     for j in range(TILES):
-        w = min(128, HANDS - 128 * j)
-        mine_ref[j, :, 0:w] = share[:, 128 * j : 128 * j + w]
+        mine_ref[j] = share[:, 128 * j : 128 * (j + 1)]
 
     def other(d):
         return lax.rem(g + d, GROUP)
@@ -231,7 +246,9 @@
     for d in group_order:
         pl.when(other(d) < TILES)(copies1[d].start)
     for i in range(PART):
-        turn_ref[i] = turn[i : i + 1]
+        row, at = spare(i)
+        turn_ref[i, :, 0:WIDE] = turn[i : i + 1]
+        turn_ref[i, :, WIDE:HANDS] = turn[row : row + 1, at : at + REST]
 
     @pl.when(g < TILES)
     def _():
@@ -266,24 +283,29 @@
     for d in reversed(group_order):
         pl.when(other(GROUP - d) < TILES)(copies3[d].wait_recv)
     for j in range(TILES):
-        w = min(128, HANDS - 128 * j)
-        root_ref[:, 128 * j : 128 * j + w] = in3_ref[j, :, 0:w]
+        root_ref[:, 128 * j : 128 * (j + 1)] = in3_ref[j, 0:PART, :]
+    for i in range(PART):
+        row, at = spare(i)
+        root_ref[i : i + 1, WIDE : WIDE + 128] = in3_ref[at // 128, row : row + 1, :]
+        root_ref[i : i + 1, WIDE + 128 : HANDS] = in3_ref[at // 128 + 1, row : row + 1, 0 : REST - 128]
 
 
 def body(
     board_cards, hand_ranks, river_count, reach_in, strategy, parent_node, pot_size, flop_weight
 ):
     tab = jnp.asarray(np.stack(np.triu_indices(52, 1)), jnp.int32)
-    slab = (PART, HANDS)
-    tile = (PART, 128)
+    slab = (8, WIDE)
+    tile = (8, 128)
     vm, dma = pltpu.VMEM, pltpu.SemaphoreType.DMA
     scratch = [
+        pltpu.SMEM((5, 1, RIVERS), jnp.int32),
         vm((RIVERS, 1, HANDS), jnp.int32),
         vm((NX, PART, HANDS), bf16),
         vm((RIVERS, LEAF, HANDS), bf16),
         vm((1, LEAF), jnp.int32),
         vm((1, LEAF), f32),
         vm((2, HANDS), jnp.int32),
+        vm((HANDS, HANDS), bf16),
         vm((HANDS, HANDS), bf16),
         vm((8, HANDS), f32),
         vm((HANDS, 8), f32),
@@ -305,12 +327,12 @@
         vm(tile, f32),
         vm((GROUP,) + tile, f32),
     ]
-    sems = (6, NX, NX) + (RIVERS,) * 6 + (NX, NX, GROUP, GROUP, NZ, NZ, GROUP, GROUP)
+    sems = (7, NX, NX) + (RIVERS,) * 6 + (NX, NX, GROUP, GROUP, NZ, NZ, GROUP, GROUP)
     turn, root = pl.pallas_call(
         river_kernel,
         name="river_values",
-        out_shape=(jax.ShapeDtypeStruct((PART, 1, HANDS), f32), jax.ShapeDtypeStruct(slab, f32)),
-        in_specs=[SM, SM, SM] + [HBM] * 6,
+        out_shape=(jax.ShapeDtypeStruct((PART, 1, HANDS), f32), jax.ShapeDtypeStruct((PART, HANDS), f32)),
+        in_specs=[HBM, SM, SM] + [HBM] * 6,
         out_specs=(VM, VM),
         scratch_shapes=scratch + [pltpu.SemaphoreType.REGULAR] * 3 + [dma((n,)) for n in sems],
         compiler_params=pltpu.CompilerParams(

time: 62.5 us -> 60.8 us (0.973)
  Pallas kernels: 58.2 us -> 56.6 us
    pallas_call x1, Pallas kernels: 58.2 us -> 56.6 us  [body(): pl.pallas_call(river_kernel, name='river_values', out_shape=(jax.ShapeDty...]
where the time goes in v4:
time: 60.8 us; the launch traced here: 60.5 us
  Pallas kernels  56.6 us (93%)
  local copies, waits for them, and re-layouts  2.02 us (3%)
  between operations  1.94 us (3%)
    pallas_call x1, Pallas kernels, body(): pl.pallas_call(river_kernel, name='river_values', out_shape=(jax.ShapeDty...  56.6 us
    unnamed x4, local copies, waits for them, and re-layouts  2.02 us

profile of v4, /device:TPU:1, one launch (start us, length us, event | category | flops | bytes accessed | tf_op | source)
XLA Modules:
  0.0 60.5 jit_solution(7743036022687584050)
XLA Ops:
  1.9 56.6 %river_values.1 = (f32[6,1,1326]{2,1,0:T(1,128)}, f32[6,1326]{1,0:T(8,128)}) custom-call(s32[5,1,6]{2,1,0:T(1,128)} %bitcast.7, s32[1]{0:T(128)S(6)} %copy.13.count_ref, f32[1]{0:T(128)S(6)} %copy.14.weight_ref, s32[6,1,1326]{2,1,0:T(1,128)} %bitcast.5, bf16[1,6,1326]{2,1,0:T(8,128)(2,1)} %reach_hbm.1, bf16[1,6,48,1326]{3,2,1,0:T(8,128)(2,1)} %strat_hbm.1, ...), custom_call_target="tpu_custom_call" | custom-call | tf_op jit(solution)/shard_map/river_values/pallas_call | solution.py:331
  58.5 0.0 copy-start
  58.5 1.4 %copy.15 = f32[1,6,1326]{2,0,1:T(1,128)} copy(f32[1,6,1326]{2,0,1:T(1,128)} %bitcast.6) | data formatting | bytes 63648
  59.9 0.0 copy-done
  59.9 0.6 %copy.16 = f32[6,1326]{1,0:T(8,128)} copy(f32[6,1326]{1,0:T(8,128)S(1)} %copy-done) | data formatting | bytes 63648
Async XLA Ops:
  58.5 1.4 %copy-start = (f32[6,1326]{1,0:T(8,128)S(1)}, f32[6,1326]{1,0:T(8,128)}, u32[]{:S(2)}) copy-start(f32[6,1326]{1,0:T(8,128)} %get-tuple-element.9) | copy-start | bytes 95476

commit v5 on v4

--- a/solution.py
+++ b/solution.py
@@ -11,7 +11,7 @@
 GROUP = NY * NC
 SLOTS = 8 * NODES
 PART = NODES // NX
-WIDE = 1152
+WIDE = 1024
 REST = HANDS - WIDE
 TILES = WIDE // 128
 lowest = -1000000000.0
@@ -57,7 +57,7 @@
 
 
 CHUNK = 256
-CHUNKS = [(j, CHUNK) for j in range(0, 1024, CHUNK)] + [(1024, 128), (WIDE, REST)]
+CHUNKS = [(j, CHUNK) for j in range(0, WIDE, CHUNK)] + [(WIDE, REST)]
 
 
 def far_first(n, width=1):
@@ -76,7 +76,6 @@
         )
         mask_ref[:, j : j + w] = (1.0 - jnp.minimum(shared, 1.0)).astype(bf16)
     count = jnp.full((1, HANDS), count_ref[0], jnp.int32)
-    share = 1.0 / (HANDS * count.astype(f32))
     for r in range(RIVERS):
         row_ref[r : r + 1, :] = rank_ref[r].astype(f32)
         hit = jnp.zeros((1, HANDS), jnp.bool_)
@@ -84,7 +83,7 @@
             hit = hit | (low == cards_ref[i, 0, r]) | (high == cards_ref[i, 0, r])
         live = jnp.where(hit, 0.0, 1.0)
         scale_ref[r : r + 1, :] = live
-        scale_ref[8 + r : 9 + r, :] = live * jnp.where(count > r, share, 0.0)
+        scale_ref[8 + r : 9 + r, :] = live * jnp.where(count > r, 1.0 / HANDS, 0.0)
     col_ref[...] = row_ref[...].T
     for r in range(RIVERS):
         colb_ref[r] = jnp.broadcast_to(col_ref[:, r : r + 1], (HANDS, 128))
@@ -105,11 +104,11 @@
 
 
 def spare(i):
-    return PART + i // 4, i % 4 * 256
+    return PART + i // 3, i % 3 * REST
 
 
 def payoff(r, j, w, row_ref, colb_ref, mask_ref):
-    col = jnp.concatenate([colb_ref[r]] * (CHUNK // 128), axis=1)
+    col = jnp.concatenate([colb_ref[r]] * 3, axis=1)
     gap = row_ref[r : r + 1, j : j + w] - col[:, :w]
     return jnp.clip(gap, -1.0, 1.0).astype(bf16) * mask_ref[:, j : j + w]
 
@@ -120,7 +119,7 @@
     cards_ref, rank_ref, reach_ref, strat_ref, parent_ref, pot_ref, tab_ref,
     pay_ref, mask_ref, row_ref, col_ref, colb_ref, scale_ref, oh_ref, potb_ref, biasb_ref,
     part_ref, relay_ref, comb_ref, back_ref, ahead_ref, last_ref,
-    mine_ref, in1_ref, sum1_ref, in2_ref, sum2_ref, in3_ref,
+    flat_ref, mine_ref, in1_ref, sum1_ref, in2_ref, sum2_ref, in3_ref,
     known_y, known_z, known_far, local, sg, rg, sa, ra, sb, rb, sc, rc, sl, rl, s1, r1, s2, r2, s3, r3,
 ):
     x = lax.axis_index("seq")
@@ -158,8 +157,8 @@
     for copy in copies:
         copy.wait()
     reach = jnp.concatenate([reach_ref[i].astype(f32) for i in range(NX)], axis=0)
-    pot2 = jnp.concatenate([potb_ref[...]] * (CHUNK // 128), axis=1)
-    bias2 = jnp.concatenate([biasb_ref[...]] * (CHUNK // 128), axis=1)
+    pot2 = jnp.concatenate([potb_ref[...]] * 3, axis=1)
+    bias2 = jnp.concatenate([biasb_ref[...]] * 3, axis=1)
 
     def river(r):
         leaf = jnp.dot(oh_ref[...], strat_ref[r], preferred_element_type=f32).reshape(8, NODES, HANDS)
@@ -231,7 +230,7 @@
         copy.wait_recv()
     best = jnp.maximum(part_ref[x, end], jnp.maximum(last_ref[0], jnp.maximum(last_ref[1], last_ref[2])))
     turn = total + best
-    share = turn * (weight_ref[0] / (NY * NZ * NC))
+    share = turn * (weight_ref[0] / count_ref[0].astype(f32))
     for j in range(TILES):
         mine_ref[j] = share[:, 128 * j : 128 * (j + 1)]
 
@@ -245,10 +244,11 @@
     copies3 = {d: move(sum2_ref, in3_ref.at[g], s3.at[d], r3.at[d], group_peer(d)) for d in group_order}
     for d in group_order:
         pl.when(other(d) < TILES)(copies1[d].start)
+    flat_ref[...] = turn
     for i in range(PART):
         row, at = spare(i)
         turn_ref[i, :, 0:WIDE] = turn[i : i + 1]
-        turn_ref[i, :, WIDE:HANDS] = turn[row : row + 1, at : at + REST]
+        turn_ref[i, :, WIDE:HANDS] = flat_ref[row : row + 1, at : at + REST]
 
     @pl.when(g < TILES)
     def _():
@@ -284,10 +284,10 @@
         pl.when(other(GROUP - d) < TILES)(copies3[d].wait_recv)
     for j in range(TILES):
         root_ref[:, 128 * j : 128 * (j + 1)] = in3_ref[j, 0:PART, :]
+        flat_ref[PART:8, 128 * j : 128 * (j + 1)] = in3_ref[j, PART:8, :]
     for i in range(PART):
         row, at = spare(i)
-        root_ref[i : i + 1, WIDE : WIDE + 128] = in3_ref[at // 128, row : row + 1, :]
-        root_ref[i : i + 1, WIDE + 128 : HANDS] = in3_ref[at // 128 + 1, row : row + 1, 0 : REST - 128]
+        root_ref[i : i + 1, WIDE:HANDS] = flat_ref[row : row + 1, at : at + REST]
 
 
 def body(
@@ -320,6 +320,7 @@
         vm((RIVERS,) + slab, f32),
         vm((RIVERS,) + slab, f32),
         vm((NX - 1,) + slab, f32),
+        vm(slab, f32),
         vm((GROUP,) + tile, f32),
         vm((GROUP,) + tile, f32),
         vm(tile, f32),
@@ -349,7 +350,7 @@
         pot_size[None, :],
         tab,
     )
-    return (jnp.transpose(turn, (1, 0, 2)), root)
+    return (jnp.transpose(turn, (1, 0, 2)) / river_count[0].astype(f32), root / (NY * NZ * NC))
 
 
 def solution(mesh):

time: 60.8 us -> 60.5 us (level)
  other arithmetic: 0 us -> 2.03 us
  local copies, waits for them, and re-layouts: 2.02 us -> 0.01 us
    div x0 -> x2, other arithmetic: none -> 2.03 us  [the longest x1 1.41 us: body(): jnp.transpose(turn, (1, 0, 2)) / river_count[0].astype(f32)]
    unnamed x4 -> x2, local copies, waits for them, and re-layouts: 2.02 us -> 0.01 us
where the time goes in v5:
time: 60.5 us; the launch traced here: 60.2 us
  Pallas kernels  56.3 us (93%)
  other arithmetic  2.03 us (3%)
  between operations  1.94 us (3%)
    pallas_call x1, Pallas kernels, body(): pl.pallas_call(river_kernel, name='river_values', out_shape=(jax.ShapeDty...  56.3 us
    div x1, other arithmetic, body(): jnp.transpose(turn, (1, 0, 2)) / river_count[0].astype(f32)  1.41 us

profile of v5, /device:TPU:1, one launch (start us, length us, event | category | flops | bytes accessed | tf_op | source)
XLA Modules:
  0.0 60.2 jit_solution(11967319011803670601)
XLA Ops:
  1.9 56.3 %river_values.1 = (f32[6,1,1326]{2,1,0:T(1,128)}, f32[6,1326]{1,0:T(8,128)}) custom-call(s32[5,1,6]{2,1,0:T(1,128)} %bitcast.8, s32[1]{0:T(128)S(6)} %copy.11.count_ref, f32[1]{0:T(128)S(6)} %copy.12.weight_ref, s32[6,1,1326]{2,1,0:T(1,128)} %bitcast.7, bf16[1,6,1326]{2,1,0:T(8,128)(2,1)} %reach_hbm.1, bf16[1,6,48,1326]{3,2,1,0:T(8,128)(2,1)} %strat_hbm.1, ...), custom_call_target="tpu_custom_call" | custom-call | tf_op jit(solution)/shard_map/river_values/pallas_call | solution.py:332
  58.2 0.0 copy-start
  58.2 1.4 %divide_bitcast_fusion = f32[1,6,1326]{2,0,1:T(1,128)} fusion(f32[6,1,1326]{2,1,0:T(1,128)} %get-tuple-element.4, f32[]{:T(128)} %bitcast.4), kind=kLoop, calls=%fused_computation | loop fusion | flops 7956 | bytes 63652 | tf_op jit(solution)/shard_map/div | solution.py:353
  59.6 0.0 copy-done
  59.6 0.6 %broadcast_multiply_fusion = f32[6,1326]{1,0:T(8,128)} fusion(f32[6,1326]{1,0:T(8,128)S(1)} %copy-done), kind=kLoop, calls=%fused_computation.1 | loop fusion | flops 7956 | bytes 63648 | tf_op jit(solution)/shard_map/div | solution.py:353
Async XLA Ops:
  58.2 1.4 %copy-start = (f32[6,1326]{1,0:T(8,128)S(1)}, f32[6,1326]{1,0:T(8,128)}, u32[]{:S(2)}) copy-start(f32[6,1326]{1,0:T(8,128)} %get-tuple-element.5) | copy-start | bytes 95476

commit v6 on v5

--- a/solution.py
+++ b/solution.py
@@ -110,7 +110,7 @@
 def payoff(r, j, w, row_ref, colb_ref, mask_ref):
     col = jnp.concatenate([colb_ref[r]] * 3, axis=1)
     gap = row_ref[r : r + 1, j : j + w] - col[:, :w]
-    return jnp.clip(gap, -1.0, 1.0).astype(bf16) * mask_ref[:, j : j + w]
+    return jnp.clip(gap.astype(bf16), -1.0, 1.0) * mask_ref[:, j : j + w]
 
 
 def river_kernel(

time: 60.5 us -> 60.4 us (level)
  no operation moved by 1% of the time
where the time goes in v6:
time: 60.4 us; the launch traced here: 60.2 us
  Pallas kernels  56.2 us (93%)
  other arithmetic  2.03 us (3%)
  between operations  1.94 us (3%)
    pallas_call x1, Pallas kernels, body(): pl.pallas_call(river_kernel, name='river_values', out_shape=(jax.ShapeDty...  56.2 us
    div x1, other arithmetic, body(): jnp.transpose(turn, (1, 0, 2)) / river_count[0].astype(f32)  1.41 us

profile of v6, /device:TPU:1, one launch (start us, length us, event | category | flops | bytes accessed | tf_op | source)
XLA Modules:
  0.0 60.2 jit_solution(8915878715200105202)
XLA Ops:
  1.9 56.2 %river_values.1 = (f32[6,1,1326]{2,1,0:T(1,128)}, f32[6,1326]{1,0:T(8,128)}) custom-call(s32[5,1,6]{2,1,0:T(1,128)} %bitcast.8, s32[1]{0:T(128)S(6)} %copy.11.count_ref, f32[1]{0:T(128)S(6)} %copy.12.weight_ref, s32[6,1,1326]{2,1,0:T(1,128)} %bitcast.7, bf16[1,6,1326]{2,1,0:T(8,128)(2,1)} %reach_hbm.1, bf16[1,6,48,1326]{3,2,1,0:T(8,128)(2,1)} %strat_hbm.1, ...), custom_call_target="tpu_custom_call" | custom-call | tf_op jit(solution)/shard_map/river_values/pallas_call | solution.py:332
  58.1 0.0 copy-start
  58.1 1.4 %divide_bitcast_fusion = f32[1,6,1326]{2,0,1:T(1,128)} fusion(f32[6,1,1326]{2,1,0:T(1,128)} %get-tuple-element.4, f32[]{:T(128)} %bitcast.4), kind=kLoop, calls=%fused_computation | loop fusion | flops 7956 | bytes 63652 | tf_op jit(solution)/shard_map/div | solution.py:353
  59.5 0.0 copy-done
  59.5 0.6 %broadcast_multiply_fusion = f32[6,1326]{1,0:T(8,128)} fusion(f32[6,1326]{1,0:T(8,128)S(1)} %copy-done), kind=kLoop, calls=%fused_computation.1 | loop fusion | flops 7956 | bytes 63648 | tf_op jit(solution)/shard_map/div | solution.py:353
Async XLA Ops:
  58.1 1.4 %copy-start = (f32[6,1326]{1,0:T(8,128)S(1)}, f32[6,1326]{1,0:T(8,128)}, u32[]{:S(2)}) copy-start(f32[6,1326]{1,0:T(8,128)} %get-tuple-element.5) | copy-start | bytes 95476
